TPU v7x, 128 devices: a whole 4x4x4 slice. The times are simulated.
128 devices in a mesh: tm: 16 (over z, x), pack: 8 (over y, core).
Axes of the slice: x: 4, y: 4, z: 4, core: 2. Of those that a mesh axis runs over, the one named last changes fastest.
Arguments:
- queries: bfloat16 [8, 8192, 1024], P('pack', 'tm'), may hold values from -8 to 8
- keys: bfloat16 [8, 8192, 1024], P('pack', 'tm'), may hold values from -8 to 8
- values: bfloat16 [8, 8192, 1024], P('pack', 'tm'), may hold values from -6 to 6
- w_out: bfloat16 [1024, 1024], replicated, may hold values from -0.1875 to 0.1875
- norm_gain: float32 [1024], replicated, may hold values from 0.1 to 1.9
- block_owner: int32 [8, 64, 1], P('pack', 'tm'), may hold values from 0 to 7; in each aligned block of 4 rows (0 to 3, 4 to 7, ..., all dimensions but the last counted through in order) at most 2 rows name the same one
- block_base: int32 [8, 64], P('pack', 'tm'), may hold values from 0 to 112
- frame_offset: int32 [8, 64, 128], P('pack', 'tm'), may hold values from 0 to 15, never falling along the last dimension, each value on 1 to 16 neighbouring positions
Outputs:
- encoded: bfloat16 [8, 8192, 1024], P('pack', 'tm')
- pooled: bfloat16 [8, 2048, 1024], P('pack', 'tm')
Inputs may be any that keep to these rules, and one draw needn't show every extreme that they name: `block_owner`: among the 4 blocks of one device (aligned runs of the list), at most 2 name the same owner. `frame_offset`: within each block of 128 frames the offsets never fall and each of 0 to 15 occurs.
All inputs are finite; a program needn't handle non-finite values.
Results may differ from a plain program's by a relative error of at most 0.008.
Values may be sent and summed in bfloat16 or wider, within the bound.
A program may use at most 128 MiB of HBM per device.

v0:
```python
import jax
import jax.numpy as jnp
from jax import lax
from jax.sharding import PartitionSpec as P

HEADS = 16
LANDMARKS = 256
BLOCK = 128
POOL_DEV = 128


def mix_heads(query_rows, mark_keys, mark_values, head_count):
    row_count, model_width = query_rows.shape
    head_dim = model_width // head_count
    query_heads = query_rows.reshape(row_count, head_count, head_dim)
    key_heads = mark_keys.reshape(-1, head_count, head_dim)
    value_heads = mark_values.reshape(-1, head_count, head_dim)
    scores = jnp.einsum(
        "nhe,mhe->nhm", query_heads, key_heads, preferred_element_type=jnp.float32
    ) * head_dim ** (-0.5)
    weights = jnp.exp(scores - jnp.max(scores, axis=-1, keepdims=True))
    totals = jnp.sum(weights, axis=-1)
    blended = jnp.einsum(
        "nhm,mhe->nhe",
        weights.astype(jnp.bfloat16),
        value_heads,
        preferred_element_type=jnp.float32,
    )
    return (blended / totals[..., None]).reshape(row_count, model_width).astype(jnp.bfloat16)


def local(queries, keys, values, w_out, norm_gain, block_owner, block_base, frame_offset):
    frame_q = queries[0]
    frame_k = keys[0]
    frame_v = values[0]
    frame_count, model_width = frame_q.shape
    span = frame_count // LANDMARKS
    mark_queries = jnp.mean(
        frame_q.reshape(LANDMARKS, span, model_width), axis=1, dtype=jnp.float32
    ).astype(jnp.bfloat16)
    mark_keys = jnp.mean(
        frame_k.reshape(LANDMARKS, span, model_width), axis=1, dtype=jnp.float32
    ).astype(jnp.bfloat16)
    mark_values = mix_heads(mark_queries, frame_k, frame_v, HEADS)
    head_dim = model_width // HEADS
    query_heads = frame_q.reshape(frame_count, HEADS, head_dim)

    def absorb(running, piece_keys, piece_values):
        running_top, running_sum, running_acc = running
        key_heads = piece_keys.reshape(-1, HEADS, head_dim)
        value_heads = piece_values.reshape(-1, HEADS, head_dim)
        scores = jnp.einsum(
            "nhe,mhe->nhm", query_heads, key_heads, preferred_element_type=jnp.float32
        ) * head_dim ** (-0.5)
        new_top = jnp.maximum(running_top, jnp.max(scores, axis=-1))
        weights = jnp.exp(scores - new_top[..., None])
        rescale = jnp.exp(running_top - new_top)
        running_sum = running_sum * rescale + jnp.sum(weights, axis=-1)
        running_acc = running_acc * rescale[..., None] + jnp.einsum(
            "nhm,mhe->nhe",
            weights.astype(jnp.bfloat16),
            value_heads,
            preferred_element_type=jnp.float32,
        )
        return (new_top, running_sum, running_acc)

    start_state = (
        jnp.full((frame_count, HEADS), -1e30, jnp.float32),
        jnp.zeros((frame_count, HEADS), jnp.float32),
        jnp.zeros((frame_count, HEADS, head_dim), jnp.float32),
    )
    running = start_state
    piece_keys = lax.all_gather(mark_keys, "tm", axis=0, tiled=True)
    piece_values = lax.all_gather(mark_values, "tm", axis=0, tiled=True)
    stacked = (
        piece_keys.reshape(-1, LANDMARKS, model_width),
        piece_values.reshape(-1, LANDMARKS, model_width),
    )

    def advance(inner_state, sub_block):
        return (absorb(inner_state, sub_block[0], sub_block[1]), None)

    running, unused = lax.scan(advance, running, stacked)
    final_top, final_sum, final_acc = running
    attended = (
        (final_acc / final_sum[..., None]).reshape(frame_count, model_width).astype(jnp.bfloat16)
    )
    projected = jnp.dot(attended, w_out, preferred_element_type=jnp.float32)
    scaled = projected * lax.rsqrt(jnp.mean(projected * projected, axis=-1, keepdims=True) + 1e-06)
    encoded = (scaled * norm_gain).astype(jnp.bfloat16)
    pack_count = lax.axis_size("pack")
    owners = block_owner[0, :, 0]
    block_count = owners.shape[0]
    slot_count = max(2, 2 * block_count // pack_count)
    pack_range = jnp.arange(pack_count, dtype=jnp.int32)
    dest_hits = (owners[:, None] == pack_range[None, :]).astype(jnp.int32)
    slot_rank = jnp.sum((jnp.cumsum(dest_hits, axis=0) - dest_hits) * dest_hits, axis=1)
    chosen = (owners[None, None, :] == pack_range[:, None, None]) & (
        slot_rank[None, None, :] == jnp.arange(slot_count, dtype=jnp.int32)[None, :, None]
    )
    filled = jnp.any(chosen, axis=-1)
    source_block = jnp.sum(
        chosen.astype(jnp.int32) * jnp.arange(block_count, dtype=jnp.int32)[None, None, :], axis=-1
    )
    frame_blocks = encoded.reshape(block_count, BLOCK, model_width)
    offsets = frame_offset[0]
    block_bases = block_base[0]
    sent_rows = jnp.where(
        filled[..., None, None],
        jnp.take(frame_blocks, source_block, axis=0),
        jnp.zeros((), jnp.bfloat16),
    )
    row_targets = jnp.take(block_bases, source_block)[..., None] + jnp.take(
        offsets, source_block, axis=0
    )
    sent_targets = jnp.where(filled[..., None], row_targets, -1).astype(jnp.bfloat16)
    got_rows, got_targets = (
        lax.all_to_all(sent_rows, "pack", split_axis=0, concat_axis=0, tiled=True),
        lax.all_to_all(sent_targets, "pack", split_axis=0, concat_axis=0, tiled=True),
    )
    pool_rows = jnp.arange(POOL_DEV, dtype=jnp.int32).astype(jnp.bfloat16)
    placing = got_targets[:, :, None, :] == pool_rows[None, None, :, None]
    pool_sums = jnp.einsum(
        "scrf,scfd->rd", placing.astype(jnp.bfloat16), got_rows, preferred_element_type=jnp.float32
    )
    pool_counts = jnp.sum(placing.astype(jnp.float32), axis=(0, 1, 3))
    pooled = (pool_sums / jnp.maximum(pool_counts, 1.0)[:, None]).astype(jnp.bfloat16)
    return (encoded[None], pooled[None])


def solution(mesh):
    return jax.shard_map(
        local,
        mesh=mesh,
        in_specs=(
            P("pack", "tm", None),
            P("pack", "tm", None),
            P("pack", "tm", None),
            P(),
            P(),
            P("pack", "tm", None),
            P("pack", "tm"),
            P("pack", "tm", None),
        ),
        out_specs=(P("pack", "tm", None), P("pack", "tm", None)),
        check_vma=False,
    )
```

profile of v0, /device:TPU:1, one launch (start us, length us, event | category | flops | bytes accessed | tf_op | source)
XLA Modules:
  0.0 595.5 jit_solution(14726853507628708703)
XLA Ops:
  45.9 6.0 %all-to-all-start = ((bf16[8,2,128]{2,1,0:T(2,128)(2,1)}), bf16[8,2,128]{2,1,0:T(2,128)(2,1)S(1)}, u32[]{:S(2)}, u32[]{:S(2)}) async-start(bf16[8,2,128]{2,1,0:T(2,128)(2,1)} %select_convert_fusion), calls=%async_computation | async-start | bytes 8192 | tf_op jit(solution)/shard_map/all_to_all | solution.py:119
  53.2 54.2 %all-gather.5.cloned.1.call-done = bf16[4096,1024]{1,0:T(8,128)(2,1)} async-done(((bf16[256,1024]{1,0:T(8,128)(2,1)}), bf16[4096,1024]{1,0:T(8,128)(2,1)}) %all-gather.5.cloned.1.call-update) | async-done | bytes 8388624 | tf_op jit(solution)/shard_map/all_gather | solution.py:74
  107.4 72.6 %all-gather.3.cloned.1.call-done = bf16[4096,1024]{1,0:T(8,128)(2,1)} async-done(((bf16[256,1024]{1,0:T(8,128)(2,1)}), bf16[4096,1024]{1,0:T(8,128)(2,1)}) %all-gather.3.cloned.1.call-update) | async-done | bytes 8388624 | tf_op jit(solution)/shard_map/all_gather | solution.py:73
  180.1 338.5 %while.15 = (s32[]{:T(128)}, f32[512,16]{0,1:T(8,128)S(1)}, f32[512,16]{0,1:T(8,128)S(1)}, f32[512,16,64]{0,2,1:T(8,128)}, bf16[16,256,1024]{2,1,0:T(8,128)(2,1)...) while((s32[]{:T(128)}, f32[512,16]{0,1:T(8,128)S(1)}, ...), condition=%wide.region_7.8_spmd.clone, body=%wide.region_4.7_spmd.clone.sunk | while | flops 555261952 | bytes 36175980 | solution.py:83
  183.4 5.8 bitcast_reduce_fusion.3
  194.2 6.5 %bitcast_add_fusion.2 = f32[512,16,64]{0,2,1:T(8,128)} fusion(f32[512,16,64]{0,2,1:T(8,128)} %get-tuple-element.187, bf16[256,16,64]{0,2,1:T(8,128)(2,1)S(1)} %bitcast.93, f32[16,256,512]{2,1,0:T(8,128)} %get-tuple-element.171, f32[512,16]{0,1:T(8,128)S(1)} %select_maximum_fusion.2, f32[512,16]{0,1:T(8,128)S(1)} %get-tuple-element.174, pred[]{:T(512)S(6)} %compare.3), kind=kOutput, calls=%fused_computation.11.clone.1 | convolution fusion | flops 276299776 | bytes 13172737 | tf_op jit(solution)/shard_map/while/body/eval_jaxpr/nhm,mhe->nhe/dot_general | solution.py:59
  214.8 7.1 %bitcast_add_fusion.2 = f32[512,16,64]{0,2,1:T(8,128)} fusion(f32[512,16,64]{0,2,1:T(8,128)} %get-tuple-element.187, bf16[256,16,64]{0,2,1:T(8,128)(2,1)S(1)} %bitcast.93, f32[16,256,512]{2,1,0:T(8,128)} %get-tuple-element.171, f32[512,16]{0,1:T(8,128)S(1)} %select_maximum_fusion.2, f32[512,16]{0,1:T(8,128)S(1)} %get-tuple-element.174, pred[]{:T(512)S(6)} %compare.3), kind=kOutput, calls=%fused_computation.11.clone.1 | convolution fusion | flops 276299776 | bytes 13172737 | tf_op jit(solution)/shard_map/while/body/eval_jaxpr/nhm,mhe->nhe/dot_general | solution.py:59
  225.2 5.8 bitcast_reduce_fusion.3
  236.0 7.1 %bitcast_add_fusion.2 = f32[512,16,64]{0,2,1:T(8,128)} fusion(f32[512,16,64]{0,2,1:T(8,128)} %get-tuple-element.187, bf16[256,16,64]{0,2,1:T(8,128)(2,1)S(1)} %bitcast.93, f32[16,256,512]{2,1,0:T(8,128)} %get-tuple-element.171, f32[512,16]{0,1:T(8,128)S(1)} %select_maximum_fusion.2, f32[512,16]{0,1:T(8,128)S(1)} %get-tuple-element.174, pred[]{:T(512)S(6)} %compare.3), kind=kOutput, calls=%fused_computation.11.clone.1 | convolution fusion | flops 276299776 | bytes 13172737 | tf_op jit(solution)/shard_map/while/body/eval_jaxpr/nhm,mhe->nhe/dot_general | solution.py:59
  246.4 5.8 bitcast_reduce_fusion.3
  257.2 7.1 %bitcast_add_fusion.2 = f32[512,16,64]{0,2,1:T(8,128)} fusion(f32[512,16,64]{0,2,1:T(8,128)} %get-tuple-element.187, bf16[256,16,64]{0,2,1:T(8,128)(2,1)S(1)} %bitcast.93, f32[16,256,512]{2,1,0:T(8,128)} %get-tuple-element.171, f32[512,16]{0,1:T(8,128)S(1)} %select_maximum_fusion.2, f32[512,16]{0,1:T(8,128)S(1)} %get-tuple-element.174, pred[]{:T(512)S(6)} %compare.3), kind=kOutput, calls=%fused_computation.11.clone.1 | convolution fusion | flops 276299776 | bytes 13172737 | tf_op jit(solution)/shard_map/while/body/eval_jaxpr/nhm,mhe->nhe/dot_general | solution.py:59
  267.6 5.8 bitcast_reduce_fusion.3
  278.4 7.1 %bitcast_add_fusion.2 = f32[512,16,64]{0,2,1:T(8,128)} fusion(f32[512,16,64]{0,2,1:T(8,128)} %get-tuple-element.187, bf16[256,16,64]{0,2,1:T(8,128)(2,1)S(1)} %bitcast.93, f32[16,256,512]{2,1,0:T(8,128)} %get-tuple-element.171, f32[512,16]{0,1:T(8,128)S(1)} %select_maximum_fusion.2, f32[512,16]{0,1:T(8,128)S(1)} %get-tuple-element.174, pred[]{:T(512)S(6)} %compare.3), kind=kOutput, calls=%fused_computation.11.clone.1 | convolution fusion | flops 276299776 | bytes 13172737 | tf_op jit(solution)/shard_map/while/body/eval_jaxpr/nhm,mhe->nhe/dot_general | solution.py:59
  288.8 5.8 bitcast_reduce_fusion.3
  299.6 7.1 %bitcast_add_fusion.2 = f32[512,16,64]{0,2,1:T(8,128)} fusion(f32[512,16,64]{0,2,1:T(8,128)} %get-tuple-element.187, bf16[256,16,64]{0,2,1:T(8,128)(2,1)S(1)} %bitcast.93, f32[16,256,512]{2,1,0:T(8,128)} %get-tuple-element.171, f32[512,16]{0,1:T(8,128)S(1)} %select_maximum_fusion.2, f32[512,16]{0,1:T(8,128)S(1)} %get-tuple-element.174, pred[]{:T(512)S(6)} %compare.3), kind=kOutput, calls=%fused_computation.11.clone.1 | convolution fusion | flops 276299776 | bytes 13172737 | tf_op jit(solution)/shard_map/while/body/eval_jaxpr/nhm,mhe->nhe/dot_general | solution.py:59
  309.9 5.8 bitcast_reduce_fusion.3
  320.8 7.1 %bitcast_add_fusion.2 = f32[512,16,64]{0,2,1:T(8,128)} fusion(f32[512,16,64]{0,2,1:T(8,128)} %get-tuple-element.187, bf16[256,16,64]{0,2,1:T(8,128)(2,1)S(1)} %bitcast.93, f32[16,256,512]{2,1,0:T(8,128)} %get-tuple-element.171, f32[512,16]{0,1:T(8,128)S(1)} %select_maximum_fusion.2, f32[512,16]{0,1:T(8,128)S(1)} %get-tuple-element.174, pred[]{:T(512)S(6)} %compare.3), kind=kOutput, calls=%fused_computation.11.clone.1 | convolution fusion | flops 276299776 | bytes 13172737 | tf_op jit(solution)/shard_map/while/body/eval_jaxpr/nhm,mhe->nhe/dot_general | solution.py:59
  331.1 5.8 bitcast_reduce_fusion.3
  342.0 7.1 %bitcast_add_fusion.2 = f32[512,16,64]{0,2,1:T(8,128)} fusion(f32[512,16,64]{0,2,1:T(8,128)} %get-tuple-element.187, bf16[256,16,64]{0,2,1:T(8,128)(2,1)S(1)} %bitcast.93, f32[16,256,512]{2,1,0:T(8,128)} %get-tuple-element.171, f32[512,16]{0,1:T(8,128)S(1)} %select_maximum_fusion.2, f32[512,16]{0,1:T(8,128)S(1)} %get-tuple-element.174, pred[]{:T(512)S(6)} %compare.3), kind=kOutput, calls=%fused_computation.11.clone.1 | convolution fusion | flops 276299776 | bytes 13172737 | tf_op jit(solution)/shard_map/while/body/eval_jaxpr/nhm,mhe->nhe/dot_general | solution.py:59
  363.2 7.1 %bitcast_add_fusion.2 = f32[512,16,64]{0,2,1:T(8,128)} fusion(f32[512,16,64]{0,2,1:T(8,128)} %get-tuple-element.187, bf16[256,16,64]{0,2,1:T(8,128)(2,1)S(1)} %bitcast.93, f32[16,256,512]{2,1,0:T(8,128)} %get-tuple-element.171, f32[512,16]{0,1:T(8,128)S(1)} %select_maximum_fusion.2, f32[512,16]{0,1:T(8,128)S(1)} %get-tuple-element.174, pred[]{:T(512)S(6)} %compare.3), kind=kOutput, calls=%fused_computation.11.clone.1 | convolution fusion | flops 276299776 | bytes 13172737 | tf_op jit(solution)/shard_map/while/body/eval_jaxpr/nhm,mhe->nhe/dot_general | solution.py:59
  373.5 5.8 bitcast_reduce_fusion.3
  384.4 7.1 %bitcast_add_fusion.2 = f32[512,16,64]{0,2,1:T(8,128)} fusion(f32[512,16,64]{0,2,1:T(8,128)} %get-tuple-element.187, bf16[256,16,64]{0,2,1:T(8,128)(2,1)S(1)} %bitcast.93, f32[16,256,512]{2,1,0:T(8,128)} %get-tuple-element.171, f32[512,16]{0,1:T(8,128)S(1)} %select_maximum_fusion.2, f32[512,16]{0,1:T(8,128)S(1)} %get-tuple-element.174, pred[]{:T(512)S(6)} %compare.3), kind=kOutput, calls=%fused_computation.11.clone.1 | convolution fusion | flops 276299776 | bytes 13172737 | tf_op jit(solution)/shard_map/while/body/eval_jaxpr/nhm,mhe->nhe/dot_general | solution.py:59
  405.5 7.1 %bitcast_add_fusion.2 = f32[512,16,64]{0,2,1:T(8,128)} fusion(f32[512,16,64]{0,2,1:T(8,128)} %get-tuple-element.187, bf16[256,16,64]{0,2,1:T(8,128)(2,1)S(1)} %bitcast.93, f32[16,256,512]{2,1,0:T(8,128)} %get-tuple-element.171, f32[512,16]{0,1:T(8,128)S(1)} %select_maximum_fusion.2, f32[512,16]{0,1:T(8,128)S(1)} %get-tuple-element.174, pred[]{:T(512)S(6)} %compare.3), kind=kOutput, calls=%fused_computation.11.clone.1 | convolution fusion | flops 276299776 | bytes 13172737 | tf_op jit(solution)/shard_map/while/body/eval_jaxpr/nhm,mhe->nhe/dot_general | solution.py:59
  415.9 5.8 bitcast_reduce_fusion.3
  426.7 7.1 %bitcast_add_fusion.2 = f32[512,16,64]{0,2,1:T(8,128)} fusion(f32[512,16,64]{0,2,1:T(8,128)} %get-tuple-element.187, bf16[256,16,64]{0,2,1:T(8,128)(2,1)S(1)} %bitcast.93, f32[16,256,512]{2,1,0:T(8,128)} %get-tuple-element.171, f32[512,16]{0,1:T(8,128)S(1)} %select_maximum_fusion.2, f32[512,16]{0,1:T(8,128)S(1)} %get-tuple-element.174, pred[]{:T(512)S(6)} %compare.3), kind=kOutput, calls=%fused_computation.11.clone.1 | convolution fusion | flops 276299776 | bytes 13172737 | tf_op jit(solution)/shard_map/while/body/eval_jaxpr/nhm,mhe->nhe/dot_general | solution.py:59
  447.9 7.1 %bitcast_add_fusion.2 = f32[512,16,64]{0,2,1:T(8,128)} fusion(f32[512,16,64]{0,2,1:T(8,128)} %get-tuple-element.187, bf16[256,16,64]{0,2,1:T(8,128)(2,1)S(1)} %bitcast.93, f32[16,256,512]{2,1,0:T(8,128)} %get-tuple-element.171, f32[512,16]{0,1:T(8,128)S(1)} %select_maximum_fusion.2, f32[512,16]{0,1:T(8,128)S(1)} %get-tuple-element.174, pred[]{:T(512)S(6)} %compare.3), kind=kOutput, calls=%fused_computation.11.clone.1 | convolution fusion | flops 276299776 | bytes 13172737 | tf_op jit(solution)/shard_map/while/body/eval_jaxpr/nhm,mhe->nhe/dot_general | solution.py:59
  458.3 5.8 bitcast_reduce_fusion.3
  469.1 7.1 %bitcast_add_fusion.2 = f32[512,16,64]{0,2,1:T(8,128)} fusion(f32[512,16,64]{0,2,1:T(8,128)} %get-tuple-element.187, bf16[256,16,64]{0,2,1:T(8,128)(2,1)S(1)} %bitcast.93, f32[16,256,512]{2,1,0:T(8,128)} %get-tuple-element.171, f32[512,16]{0,1:T(8,128)S(1)} %select_maximum_fusion.2, f32[512,16]{0,1:T(8,128)S(1)} %get-tuple-element.174, pred[]{:T(512)S(6)} %compare.3), kind=kOutput, calls=%fused_computation.11.clone.1 | convolution fusion | flops 276299776 | bytes 13172737 | tf_op jit(solution)/shard_map/while/body/eval_jaxpr/nhm,mhe->nhe/dot_general | solution.py:59
  490.3 7.1 %bitcast_add_fusion.2 = f32[512,16,64]{0,2,1:T(8,128)} fusion(f32[512,16,64]{0,2,1:T(8,128)} %get-tuple-element.187, bf16[256,16,64]{0,2,1:T(8,128)(2,1)S(1)} %bitcast.93, f32[16,256,512]{2,1,0:T(8,128)} %get-tuple-element.171, f32[512,16]{0,1:T(8,128)S(1)} %select_maximum_fusion.2, f32[512,16]{0,1:T(8,128)S(1)} %get-tuple-element.174, pred[]{:T(512)S(6)} %compare.3), kind=kOutput, calls=%fused_computation.11.clone.1 | convolution fusion | flops 276299776 | bytes 13172737 | tf_op jit(solution)/shard_map/while/body/eval_jaxpr/nhm,mhe->nhe/dot_general | solution.py:59
  500.7 5.8 bitcast_reduce_fusion.3
  511.5 7.1 %bitcast_add_fusion.2 = f32[512,16,64]{0,2,1:T(8,128)} fusion(f32[512,16,64]{0,2,1:T(8,128)} %get-tuple-element.187, bf16[256,16,64]{0,2,1:T(8,128)(2,1)S(1)} %bitcast.93, f32[16,256,512]{2,1,0:T(8,128)} %get-tuple-element.171, f32[512,16]{0,1:T(8,128)S(1)} %select_maximum_fusion.2, f32[512,16]{0,1:T(8,128)S(1)} %get-tuple-element.174, pred[]{:T(512)S(6)} %compare.3), kind=kOutput, calls=%fused_computation.11.clone.1 | convolution fusion | flops 276299776 | bytes 13172737 | tf_op jit(solution)/shard_map/while/body/eval_jaxpr/nhm,mhe->nhe/dot_general | solution.py:59
  539.2 45.8 %all-to-all-done.1 = bf16[8,2,128,1024]{3,2,1,0:T(8,128)(2,1)} async-done(((bf16[8,2,128,1024]{3,2,1,0:T(8,128)(2,1)}), bf16[8,2,128,1024]{3,2,1,0:T(8,128)(2,1)}, u32[]{:S(2)}, u32[]{:S(2)}) %all-to-all-start.1) | async-done | bytes 4194336 | tf_op jit(solution)/shard_map/all_to_all | solution.py:118
  (190 shorter events, 226.6 us)
Async XLA Ops:
  7.2 513.3 %copy-start = (bf16[1024,1024]{1,0:T(8,128)(2,1)S(1)}, bf16[1024,1024]{1,0:T(8,128)(2,1)}, u32[]{:S(2)}) copy-start(bf16[1024,1024]{1,0:T(8,128)(2,1)} %param.13) | copy-start | bytes 6291460
  7.2 12.9 %copy-start.3 = (bf16[1,512,1024]{2,1,0:T(8,128)(2,1)S(1)}, bf16[1,512,1024]{2,1,0:T(8,128)(2,1)}, u32[]{:S(2)}) copy-start(bf16[1,512,1024]{2,1,0:T(8,128)(2,1)} %param.11) | copy-start | bytes 3145732
  7.2 100.3 %all-gather.5.cloned.1.call-start = ((), (), s32[]{:S(2)}) async-start(), calls=%async_computation.3 | async-start | bytes 8912896 | tf_op jit(solution)/shard_map/all_gather | solution.py:74
  26.4 1.9 copy-start.6
  33.1 9.7 %copy-start.8 = (s32[1,4,1]{1,2,0:T(1,128)S(1)}, s32[1,4,1]{1,2,0:T(1,128)}, u32[]{:S(2)}) copy-start(s32[1,4,1]{1,2,0:T(1,128)} %param.15) | copy-start | bytes 52
  33.1 10.3 %copy-start.1 = (s32[1,4]{1,0:T(1,128)S(1)}, s32[1,4]{1,0:T(1,128)}, u32[]{:S(2)}) copy-start(s32[1,4]{1,0:T(1,128)} %param.16) | copy-start | bytes 52
  33.1 146.9 %all-gather.3.cloned.1.call-start = ((), (), s32[]{:S(2)}) async-start(), calls=%async_computation.2 | async-start | bytes 8912896 | tf_op jit(solution)/shard_map/all_gather | solution.py:73
  35.5 9.2 %copy-start.5 = (s32[1,4,128]{2,1,0:T(4,128)S(1)}, s32[1,4,128]{2,1,0:T(4,128)}, u32[]{:S(2)}) copy-start(s32[1,4,128]{2,1,0:T(4,128)} %param.17) | copy-start | bytes 6148
  35.5 16.4 %copy-start.4 = (bf16[1,512,1024]{2,1,0:T(8,128)(2,1)S(1)}, bf16[1,512,1024]{2,1,0:T(8,128)(2,1)}, u32[]{:S(2)}) copy-start(bf16[1,512,1024]{2,1,0:T(8,128)(2,1)} %param.10) | copy-start | bytes 3145732
  45.9 485.1 %all-to-all-start = ((bf16[8,2,128]{2,1,0:T(2,128)(2,1)}), bf16[8,2,128]{2,1,0:T(2,128)(2,1)S(1)}, u32[]{:S(2)}, u32[]{:S(2)}) async-start(bf16[8,2,128]{2,1,0:T(2,128)(2,1)} %select_convert_fusion), calls=%async_computation | async-start | bytes 8192 | tf_op jit(solution)/shard_map/all_to_all | solution.py:119
  518.6 4.7 copy-start.7
  521.9 1.4 copy-start.2
  531.0 54.0 %all-to-all-start.1 = ((bf16[8,2,128,1024]{3,2,1,0:T(8,128)(2,1)}), bf16[8,2,128,1024]{3,2,1,0:T(8,128)(2,1)}, u32[]{:S(2)}, u32[]{:S(2)}) async-start(bf16[8,2,128,1024]{3,2,1,0:T(8,128)(2,1)} %select_select_fusion), calls=%async_computation.1 | async-start | bytes 8388608 | tf_op jit(solution)/shard_map/all_to_all | solution.py:118
Sparse Core Ops, SparseCore 0:
  33.2 74.1 all-gather.4
  109.6 70.4 all-gather.2
where the time goes:
time: 599 us; the launch traced here: 596 us
  matrix products  215 us (36%)
  waiting for transfers between devices  173 us (29%)
  other arithmetic  105 us (18%)
  local copies, waits for them, and re-layouts  77.1 us (13%)
  between operations  14.2 us (2%)
  starting transfers between devices  11.1 us (2%)
    dot_general x16, matrix products, absorb(): jnp.einsum('nhm,mhe->nhe', weights.astype(jnp.bfloat16), value_heads, pre...  113 us
    dot_general x16, matrix products, absorb(): jnp.einsum('nhe,mhe->nhm', query_heads, key_heads, preferred_element_type...  92 us
    reduce_sum x16, other arithmetic, absorb(): running_sum = running_sum * rescale + jnp.sum(weights, axis=-1)  77.1 us
    all_gather x1, waiting for transfers between devices, local(): piece_keys = lax.all_gather(mark_keys, 'tm', axis=0, tiled=True)  72.6 us
    dynamic_slice x48, local copies, waits for them, and re-layouts, local(): running, unused = lax.scan(advance, running, stacked)  56.1 us
    all_gather x1, waiting for transfers between devices, local(): piece_values = lax.all_gather(mark_values, 'tm', axis=0, tiled=True)  54.2 us
    all_to_all x1, waiting for transfers between devices, local(): lax.all_to_all(sent_rows, 'pack', split_axis=0, concat_axis=0, tiled=True)  45.8 us
  transfers between devices with their start and end apart: 4, of which 3 were waited for; matrix products, arithmetic and copies ran while one was open for 61% of the time, Pallas kernels for 0%

commit v1 on v0

--- a/solution.py
+++ b/solution.py
@@ -1,3 +1,4 @@
+import functools
 import jax
 import jax.numpy as jnp
 from jax import lax
@@ -7,6 +8,37 @@
 LANDMARKS = 256
 BLOCK = 128
 POOL_DEV = 128
+
+
+def rest_quotas(block_in, axis_no):
+    carry_in, long_array, local_part = (
+        lax.axis_size("tm"),
+        lax.axis_index("tm"),
+        block_in.shape[axis_no],
+    )
+    fields = tuple(((ix, (ix + 1) % carry_in) for ix in range(carry_in)))
+    so_far_all = tuple(((ix, (ix - 1) % carry_in) for ix in range(carry_in)))
+    now = jnp.zeros(
+        (*block_in.shape[:axis_no], carry_in * local_part, *block_in.shape[axis_no + 1 :]),
+        block_in.dtype,
+    )
+    now = lax.dynamic_update_slice_in_dim(now, block_in, long_array * local_part, axis=axis_no)
+    odd = high = block_in
+    found_now = carry_in // 2
+    for kk in range(1, found_now + 1):
+        odd = lax.ppermute(odd, axis_name="tm", perm=fields)
+        now = lax.dynamic_update_slice_in_dim(
+            now, odd, (long_array - kk) % carry_in * local_part, axis=axis_no
+        )
+        if kk < carry_in - found_now:
+            high = lax.ppermute(high, axis_name="tm", perm=so_far_all)
+            now = lax.dynamic_update_slice_in_dim(
+                now, high, (long_array + kk) % carry_in * local_part, axis=axis_no
+            )
+    return now
+
+
+press_vector = functools.partial(rest_quotas, axis_no=0)
 
 
 def mix_heads(query_rows, mark_keys, mark_values, head_count):
@@ -70,7 +102,7 @@
         jnp.zeros((frame_count, HEADS, head_dim), jnp.float32),
     )
     running = start_state
-    piece_keys = lax.all_gather(mark_keys, "tm", axis=0, tiled=True)
+    piece_keys = press_vector(mark_keys)
     piece_values = lax.all_gather(mark_values, "tm", axis=0, tiled=True)
     stacked = (
         piece_keys.reshape(-1, LANDMARKS, model_width),

time: 599 us -> 635 us (1.060)
  starting transfers between devices: 11.1 us -> 50.9 us
  waiting for transfers between devices: 173 us -> 141 us
  local copies, waits for them, and re-layouts: 77.1 us -> 107 us
    ppermute x0 -> x15, waiting for transfers between devices: none -> 95.2 us  [the longest x8 82.2 us: rest_quotas(): odd = lax.ppermute(odd, axis_name='tm', perm=fields)]
    all_gather x1 -> x0, waiting for transfers between devices: 72.6 us -> none  [local(): piece_keys = lax.all_gather(mark_keys, 'tm', axis=0, tiled=True)]
    all_gather x1, waiting for transfers between devices: 54.2 us -> 0.01 us  [local(): piece_values = lax.all_gather(mark_values, 'tm', axis=0, tiled=True)]
    ppermute x0 -> x15, starting transfers between devices: none -> 37.2 us  [the longest x7 35.1 us: rest_quotas(): high = lax.ppermute(high, axis_name='tm', perm=so_far_all)]
    dynamic_update_slice x0 -> x15, local copies, waits for them, and re-layouts: none -> 24 us  [the longest x8 13 us: rest_quotas(): lax.dynamic_update_slice_in_dim(now, odd, (long_array - kk) % carry_in *...]
  transfers between devices with their start and end apart: 4 -> 18, of which waited for: 3 -> 11; matrix products, arithmetic and copies ran while one was open for 61% -> 62% of each run, Pallas kernels for 0% -> 0%
where the time goes in v1:
time: 635 us; the launch traced here: 632 us
  matrix products  214 us (34%)
  waiting for transfers between devices  141 us (22%)
  local copies, waits for them, and re-layouts  107 us (17%)
  other arithmetic  104 us (16%)
  starting transfers between devices  50.9 us (8%)
  between operations  14.2 us (2%)
    dot_general x16, matrix products, absorb(): jnp.einsum('nhm,mhe->nhe', weights.astype(jnp.bfloat16), value_heads, pre...  112 us
    dot_general x16, matrix products, absorb(): jnp.einsum('nhe,mhe->nhm', query_heads, key_heads, preferred_element_type...  91.9 us
    ppermute x8, waiting for transfers between devices, rest_quotas(): odd = lax.ppermute(odd, axis_name='tm', perm=fields)  82.2 us
    reduce_sum x16, other arithmetic, absorb(): running_sum = running_sum * rescale + jnp.sum(weights, axis=-1)  77.1 us
    dynamic_slice x48, local copies, waits for them, and re-layouts, local(): running, unused = lax.scan(advance, running, stacked)  56.8 us
    all_to_all x1, waiting for transfers between devices, local(): lax.all_to_all(sent_rows, 'pack', split_axis=0, concat_axis=0, tiled=True)  45.8 us
    ppermute x7, starting transfers between devices, rest_quotas(): high = lax.ppermute(high, axis_name='tm', perm=so_far_all)  35.1 us
    ppermute x7, waiting for transfers between devices, rest_quotas(): high = lax.ppermute(high, axis_name='tm', perm=so_far_all)  13 us
  transfers between devices with their start and end apart: 18, of which 11 were waited for; matrix products, arithmetic and copies ran while one was open for 62% of the time, Pallas kernels for 0%

profile of v1, /device:TPU:1, one launch (start us, length us, event | category | flops | bytes accessed | tf_op | source)
XLA Modules:
  0.0 631.5 jit_solution(5457283038239201652)
XLA Ops:
  52.6 20.0 %collective-permute-done = bf16[256,1024]{1,0:T(8,128)(2,1)S(1)} collective-permute-done((bf16[256,1024]{1,0:T(8,128)(2,1)S(1)}, bf16[256,1024]{1,0:T(8,128)(2,1)S(1)}, u32[]{:S(2)}, u32[]{:S(2)}) %collective-permute-start) | collective-permute-done | bytes 524320 | tf_op jit(solution)/shard_map/ppermute | solution.py:29
  77.3 14.7 %collective-permute-done.2 = bf16[256,1024]{1,0:T(8,128)(2,1)} collective-permute-done((bf16[256,1024]{1,0:T(8,128)(2,1)S(1)}, bf16[256,1024]{1,0:T(8,128)(2,1)}, u32[]{:S(2)}, u32[]{:S(2)}) %collective-permute-start.2) | collective-permute-done | bytes 524320 | tf_op jit(solution)/shard_map/ppermute | solution.py:29
  101.7 17.6 %collective-permute-done.4 = bf16[256,1024]{1,0:T(8,128)(2,1)} collective-permute-done((bf16[256,1024]{1,0:T(8,128)(2,1)}, bf16[256,1024]{1,0:T(8,128)(2,1)}, u32[]{:S(2)}, u32[]{:S(2)}) %collective-permute-start.4) | collective-permute-done | bytes 524320 | tf_op jit(solution)/shard_map/ppermute | solution.py:29
  128.7 15.6 %collective-permute-done.6 = bf16[256,1024]{1,0:T(8,128)(2,1)} collective-permute-done((bf16[256,1024]{1,0:T(8,128)(2,1)}, bf16[256,1024]{1,0:T(8,128)(2,1)}, u32[]{:S(2)}, u32[]{:S(2)}) %collective-permute-start.6) | collective-permute-done | bytes 524320 | tf_op jit(solution)/shard_map/ppermute | solution.py:29
  151.2 8.1 %collective-permute-done.8 = bf16[256,1024]{1,0:T(8,128)(2,1)} collective-permute-done((bf16[256,1024]{1,0:T(8,128)(2,1)}, bf16[256,1024]{1,0:T(8,128)(2,1)}, u32[]{:S(2)}, u32[]{:S(2)}) %collective-permute-start.8) | collective-permute-done | bytes 524320 | tf_op jit(solution)/shard_map/ppermute | solution.py:29
  159.9 7.2 %all-to-all-start = ((bf16[8,2,128]{2,1,0:T(2,128)(2,1)}), bf16[8,2,128]{2,1,0:T(2,128)(2,1)S(1)}, u32[]{:S(2)}, u32[]{:S(2)}) async-start(bf16[8,2,128]{2,1,0:T(2,128)(2,1)} %select_convert_fusion), calls=%async_computation | async-start | bytes 8192 | tf_op jit(solution)/shard_map/all_to_all | solution.py:151
  207.5 6.2 collective-permute-done.14
  214.6 338.7 %while.15 = (s32[]{:T(128)}, f32[512,16]{0,1:T(8,128)S(1)}, f32[512,16]{0,1:T(8,128)S(1)}, f32[512,16,64]{0,2,1:T(8,128)}, bf16[16,256,1024]{2,1,0:T(8,128)(2,1)...) while((s32[]{:T(128)}, f32[512,16]{0,1:T(8,128)S(1)}, ...), condition=%wide.region_7.8_spmd.clone, body=%wide.region_4.7_spmd.clone.sunk | while | flops 555261952 | bytes 36175980 | solution.py:115
  228.8 6.4 %bitcast_add_fusion.2 = f32[512,16,64]{0,2,1:T(8,128)} fusion(f32[512,16,64]{0,2,1:T(8,128)} %get-tuple-element.189, bf16[256,16,64]{0,2,1:T(8,128)(2,1)S(1)} %bitcast.93, f32[16,256,512]{2,1,0:T(8,128)} %get-tuple-element.173, f32[512,16]{0,1:T(8,128)S(1)} %select_maximum_fusion.2, f32[512,16]{0,1:T(8,128)S(1)} %get-tuple-element.176, pred[]{:T(512)S(6)} %compare.18), kind=kOutput, calls=%fused_computation.11.clone.1 | convolution fusion | flops 276299776 | bytes 13172737 | tf_op jit(solution)/shard_map/while/body/eval_jaxpr/nhm,mhe->nhe/dot_general | solution.py:91
  238.6 5.7 bitcast_reduce_fusion.3
  249.4 7.0 %bitcast_add_fusion.2 = f32[512,16,64]{0,2,1:T(8,128)} fusion(f32[512,16,64]{0,2,1:T(8,128)} %get-tuple-element.189, bf16[256,16,64]{0,2,1:T(8,128)(2,1)S(1)} %bitcast.93, f32[16,256,512]{2,1,0:T(8,128)} %get-tuple-element.173, f32[512,16]{0,1:T(8,128)S(1)} %select_maximum_fusion.2, f32[512,16]{0,1:T(8,128)S(1)} %get-tuple-element.176, pred[]{:T(512)S(6)} %compare.18), kind=kOutput, calls=%fused_computation.11.clone.1 | convolution fusion | flops 276299776 | bytes 13172737 | tf_op jit(solution)/shard_map/while/body/eval_jaxpr/nhm,mhe->nhe/dot_general | solution.py:91
  270.6 7.0 %bitcast_add_fusion.2 = f32[512,16,64]{0,2,1:T(8,128)} fusion(f32[512,16,64]{0,2,1:T(8,128)} %get-tuple-element.189, bf16[256,16,64]{0,2,1:T(8,128)(2,1)S(1)} %bitcast.93, f32[16,256,512]{2,1,0:T(8,128)} %get-tuple-element.173, f32[512,16]{0,1:T(8,128)S(1)} %select_maximum_fusion.2, f32[512,16]{0,1:T(8,128)S(1)} %get-tuple-element.176, pred[]{:T(512)S(6)} %compare.18), kind=kOutput, calls=%fused_computation.11.clone.1 | convolution fusion | flops 276299776 | bytes 13172737 | tf_op jit(solution)/shard_map/while/body/eval_jaxpr/nhm,mhe->nhe/dot_general | solution.py:91
  281.0 5.7 bitcast_reduce_fusion.3
  291.8 7.0 %bitcast_add_fusion.2 = f32[512,16,64]{0,2,1:T(8,128)} fusion(f32[512,16,64]{0,2,1:T(8,128)} %get-tuple-element.189, bf16[256,16,64]{0,2,1:T(8,128)(2,1)S(1)} %bitcast.93, f32[16,256,512]{2,1,0:T(8,128)} %get-tuple-element.173, f32[512,16]{0,1:T(8,128)S(1)} %select_maximum_fusion.2, f32[512,16]{0,1:T(8,128)S(1)} %get-tuple-element.176, pred[]{:T(512)S(6)} %compare.18), kind=kOutput, calls=%fused_computation.11.clone.1 | convolution fusion | flops 276299776 | bytes 13172737 | tf_op jit(solution)/shard_map/while/body/eval_jaxpr/nhm,mhe->nhe/dot_general | solution.py:91
  313.0 7.0 %bitcast_add_fusion.2 = f32[512,16,64]{0,2,1:T(8,128)} fusion(f32[512,16,64]{0,2,1:T(8,128)} %get-tuple-element.189, bf16[256,16,64]{0,2,1:T(8,128)(2,1)S(1)} %bitcast.93, f32[16,256,512]{2,1,0:T(8,128)} %get-tuple-element.173, f32[512,16]{0,1:T(8,128)S(1)} %select_maximum_fusion.2, f32[512,16]{0,1:T(8,128)S(1)} %get-tuple-element.176, pred[]{:T(512)S(6)} %compare.18), kind=kOutput, calls=%fused_computation.11.clone.1 | convolution fusion | flops 276299776 | bytes 13172737 | tf_op jit(solution)/shard_map/while/body/eval_jaxpr/nhm,mhe->nhe/dot_general | solution.py:91
  323.4 5.7 bitcast_reduce_fusion.3
  334.2 7.0 %bitcast_add_fusion.2 = f32[512,16,64]{0,2,1:T(8,128)} fusion(f32[512,16,64]{0,2,1:T(8,128)} %get-tuple-element.189, bf16[256,16,64]{0,2,1:T(8,128)(2,1)S(1)} %bitcast.93, f32[16,256,512]{2,1,0:T(8,128)} %get-tuple-element.173, f32[512,16]{0,1:T(8,128)S(1)} %select_maximum_fusion.2, f32[512,16]{0,1:T(8,128)S(1)} %get-tuple-element.176, pred[]{:T(512)S(6)} %compare.18), kind=kOutput, calls=%fused_computation.11.clone.1 | convolution fusion | flops 276299776 | bytes 13172737 | tf_op jit(solution)/shard_map/while/body/eval_jaxpr/nhm,mhe->nhe/dot_general | solution.py:91
  355.4 7.0 %bitcast_add_fusion.2 = f32[512,16,64]{0,2,1:T(8,128)} fusion(f32[512,16,64]{0,2,1:T(8,128)} %get-tuple-element.189, bf16[256,16,64]{0,2,1:T(8,128)(2,1)S(1)} %bitcast.93, f32[16,256,512]{2,1,0:T(8,128)} %get-tuple-element.173, f32[512,16]{0,1:T(8,128)S(1)} %select_maximum_fusion.2, f32[512,16]{0,1:T(8,128)S(1)} %get-tuple-element.176, pred[]{:T(512)S(6)} %compare.18), kind=kOutput, calls=%fused_computation.11.clone.1 | convolution fusion | flops 276299776 | bytes 13172737 | tf_op jit(solution)/shard_map/while/body/eval_jaxpr/nhm,mhe->nhe/dot_general | solution.py:91
  365.8 5.7 bitcast_reduce_fusion.3
  376.6 7.0 %bitcast_add_fusion.2 = f32[512,16,64]{0,2,1:T(8,128)} fusion(f32[512,16,64]{0,2,1:T(8,128)} %get-tuple-element.189, bf16[256,16,64]{0,2,1:T(8,128)(2,1)S(1)} %bitcast.93, f32[16,256,512]{2,1,0:T(8,128)} %get-tuple-element.173, f32[512,16]{0,1:T(8,128)S(1)} %select_maximum_fusion.2, f32[512,16]{0,1:T(8,128)S(1)} %get-tuple-element.176, pred[]{:T(512)S(6)} %compare.18), kind=kOutput, calls=%fused_computation.11.clone.1 | convolution fusion | flops 276299776 | bytes 13172737 | tf_op jit(solution)/shard_map/while/body/eval_jaxpr/nhm,mhe->nhe/dot_general | solution.py:91
  397.8 7.0 %bitcast_add_fusion.2 = f32[512,16,64]{0,2,1:T(8,128)} fusion(f32[512,16,64]{0,2,1:T(8,128)} %get-tuple-element.189, bf16[256,16,64]{0,2,1:T(8,128)(2,1)S(1)} %bitcast.93, f32[16,256,512]{2,1,0:T(8,128)} %get-tuple-element.173, f32[512,16]{0,1:T(8,128)S(1)} %select_maximum_fusion.2, f32[512,16]{0,1:T(8,128)S(1)} %get-tuple-element.176, pred[]{:T(512)S(6)} %compare.18), kind=kOutput, calls=%fused_computation.11.clone.1 | convolution fusion | flops 276299776 | bytes 13172737 | tf_op jit(solution)/shard_map/while/body/eval_jaxpr/nhm,mhe->nhe/dot_general | solution.py:91
  408.2 5.7 bitcast_reduce_fusion.3
  419.0 7.0 %bitcast_add_fusion.2 = f32[512,16,64]{0,2,1:T(8,128)} fusion(f32[512,16,64]{0,2,1:T(8,128)} %get-tuple-element.189, bf16[256,16,64]{0,2,1:T(8,128)(2,1)S(1)} %bitcast.93, f32[16,256,512]{2,1,0:T(8,128)} %get-tuple-element.173, f32[512,16]{0,1:T(8,128)S(1)} %select_maximum_fusion.2, f32[512,16]{0,1:T(8,128)S(1)} %get-tuple-element.176, pred[]{:T(512)S(6)} %compare.18), kind=kOutput, calls=%fused_computation.11.clone.1 | convolution fusion | flops 276299776 | bytes 13172737 | tf_op jit(solution)/shard_map/while/body/eval_jaxpr/nhm,mhe->nhe/dot_general | solution.py:91
  440.2 7.0 %bitcast_add_fusion.2 = f32[512,16,64]{0,2,1:T(8,128)} fusion(f32[512,16,64]{0,2,1:T(8,128)} %get-tuple-element.189, bf16[256,16,64]{0,2,1:T(8,128)(2,1)S(1)} %bitcast.93, f32[16,256,512]{2,1,0:T(8,128)} %get-tuple-element.173, f32[512,16]{0,1:T(8,128)S(1)} %select_maximum_fusion.2, f32[512,16]{0,1:T(8,128)S(1)} %get-tuple-element.176, pred[]{:T(512)S(6)} %compare.18), kind=kOutput, calls=%fused_computation.11.clone.1 | convolution fusion | flops 276299776 | bytes 13172737 | tf_op jit(solution)/shard_map/while/body/eval_jaxpr/nhm,mhe->nhe/dot_general | solution.py:91
  450.6 5.7 bitcast_reduce_fusion.3
  461.4 7.0 %bitcast_add_fusion.2 = f32[512,16,64]{0,2,1:T(8,128)} fusion(f32[512,16,64]{0,2,1:T(8,128)} %get-tuple-element.189, bf16[256,16,64]{0,2,1:T(8,128)(2,1)S(1)} %bitcast.93, f32[16,256,512]{2,1,0:T(8,128)} %get-tuple-element.173, f32[512,16]{0,1:T(8,128)S(1)} %select_maximum_fusion.2, f32[512,16]{0,1:T(8,128)S(1)} %get-tuple-element.176, pred[]{:T(512)S(6)} %compare.18), kind=kOutput, calls=%fused_computation.11.clone.1 | convolution fusion | flops 276299776 | bytes 13172737 | tf_op jit(solution)/shard_map/while/body/eval_jaxpr/nhm,mhe->nhe/dot_general | solution.py:91
  482.6 7.0 %bitcast_add_fusion.2 = f32[512,16,64]{0,2,1:T(8,128)} fusion(f32[512,16,64]{0,2,1:T(8,128)} %get-tuple-element.189, bf16[256,16,64]{0,2,1:T(8,128)(2,1)S(1)} %bitcast.93, f32[16,256,512]{2,1,0:T(8,128)} %get-tuple-element.173, f32[512,16]{0,1:T(8,128)S(1)} %select_maximum_fusion.2, f32[512,16]{0,1:T(8,128)S(1)} %get-tuple-element.176, pred[]{:T(512)S(6)} %compare.18), kind=kOutput, calls=%fused_computation.11.clone.1 | convolution fusion | flops 276299776 | bytes 13172737 | tf_op jit(solution)/shard_map/while/body/eval_jaxpr/nhm,mhe->nhe/dot_general | solution.py:91
  503.8 7.0 %bitcast_add_fusion.2 = f32[512,16,64]{0,2,1:T(8,128)} fusion(f32[512,16,64]{0,2,1:T(8,128)} %get-tuple-element.189, bf16[256,16,64]{0,2,1:T(8,128)(2,1)S(1)} %bitcast.93, f32[16,256,512]{2,1,0:T(8,128)} %get-tuple-element.173, f32[512,16]{0,1:T(8,128)S(1)} %select_maximum_fusion.2, f32[512,16]{0,1:T(8,128)S(1)} %get-tuple-element.176, pred[]{:T(512)S(6)} %compare.18), kind=kOutput, calls=%fused_computation.11.clone.1 | convolution fusion | flops 276299776 | bytes 13172737 | tf_op jit(solution)/shard_map/while/body/eval_jaxpr/nhm,mhe->nhe/dot_general | solution.py:91
  525.0 7.0 %bitcast_add_fusion.2 = f32[512,16,64]{0,2,1:T(8,128)} fusion(f32[512,16,64]{0,2,1:T(8,128)} %get-tuple-element.189, bf16[256,16,64]{0,2,1:T(8,128)(2,1)S(1)} %bitcast.93, f32[16,256,512]{2,1,0:T(8,128)} %get-tuple-element.173, f32[512,16]{0,1:T(8,128)S(1)} %select_maximum_fusion.2, f32[512,16]{0,1:T(8,128)S(1)} %get-tuple-element.176, pred[]{:T(512)S(6)} %compare.18), kind=kOutput, calls=%fused_computation.11.clone.1 | convolution fusion | flops 276299776 | bytes 13172737 | tf_op jit(solution)/shard_map/while/body/eval_jaxpr/nhm,mhe->nhe/dot_general | solution.py:91
  546.2 7.0 %bitcast_add_fusion.2 = f32[512,16,64]{0,2,1:T(8,128)} fusion(f32[512,16,64]{0,2,1:T(8,128)} %get-tuple-element.189, bf16[256,16,64]{0,2,1:T(8,128)(2,1)S(1)} %bitcast.93, f32[16,256,512]{2,1,0:T(8,128)} %get-tuple-element.173, f32[512,16]{0,1:T(8,128)S(1)} %select_maximum_fusion.2, f32[512,16]{0,1:T(8,128)S(1)} %get-tuple-element.176, pred[]{:T(512)S(6)} %compare.18), kind=kOutput, calls=%fused_computation.11.clone.1 | convolution fusion | flops 276299776 | bytes 13172737 | tf_op jit(solution)/shard_map/while/body/eval_jaxpr/nhm,mhe->nhe/dot_general | solution.py:91
  565.6 6.4 %all-to-all-start.1 = ((bf16[8,2,128,1024]{3,2,1,0:T(8,128)(2,1)}), bf16[8,2,128,1024]{3,2,1,0:T(8,128)(2,1)}, u32[]{:S(2)}, u32[]{:S(2)}) async-start(bf16[8,2,128,1024]{3,2,1,0:T(8,128)(2,1)} %select_select_fusion), calls=%async_computation.1 | async-start | bytes 8388608 | tf_op jit(solution)/shard_map/all_to_all | solution.py:150
  575.2 45.8 %all-to-all-done.1 = bf16[8,2,128,1024]{3,2,1,0:T(8,128)(2,1)} async-done(((bf16[8,2,128,1024]{3,2,1,0:T(8,128)(2,1)}), bf16[8,2,128,1024]{3,2,1,0:T(8,128)(2,1)}, u32[]{:S(2)}, u32[]{:S(2)}) %all-to-all-start.1) | async-done | bytes 4194336 | tf_op jit(solution)/shard_map/all_to_all | solution.py:150
  (237 shorter events, 328.8 us)
Async XLA Ops:
  7.2 548.0 %copy-start = (bf16[1024,1024]{1,0:T(8,128)(2,1)S(1)}, bf16[1024,1024]{1,0:T(8,128)(2,1)}, u32[]{:S(2)}) copy-start(bf16[1024,1024]{1,0:T(8,128)(2,1)} %param.13) | copy-start | bytes 6291460
  7.2 12.8 %copy-start.3 = (bf16[1,512,1024]{2,1,0:T(8,128)(2,1)S(1)}, bf16[1,512,1024]{2,1,0:T(8,128)(2,1)}, u32[]{:S(2)}) copy-start(bf16[1,512,1024]{2,1,0:T(8,128)(2,1)} %param.11) | copy-start | bytes 3145732
  7.2 207.4 %all-gather.2.cloned.1.call-start = ((), (), s32[]{:S(2)}) async-start(), calls=%async_computation.2 | async-start | bytes 8912896 | tf_op jit(solution)/shard_map/all_gather | solution.py:106
  23.6 4.8 copy-start.7
  33.2 58.8 %copy-start.10 = (s32[1,4,1]{1,2,0:T(1,128)S(1)}, s32[1,4,1]{1,2,0:T(1,128)}, u32[]{:S(2)}) copy-start(s32[1,4,1]{1,2,0:T(1,128)} %param.15) | copy-start | bytes 52
  33.2 111.3 %copy-start.1 = (s32[1,4]{1,0:T(1,128)S(1)}, s32[1,4]{1,0:T(1,128)}, u32[]{:S(2)}) copy-start(s32[1,4]{1,0:T(1,128)} %param.16) | copy-start | bytes 52
  35.5 110.3 %copy-start.6 = (s32[1,4,128]{2,1,0:T(4,128)S(1)}, s32[1,4,128]{2,1,0:T(4,128)}, u32[]{:S(2)}) copy-start(s32[1,4,128]{2,1,0:T(4,128)} %param.17) | copy-start | bytes 6148
  40.5 126.7 %copy-start.4 = (bf16[1,512,1024]{2,1,0:T(8,128)(2,1)S(1)}, bf16[1,512,1024]{2,1,0:T(8,128)(2,1)}, u32[]{:S(2)}) copy-start(bf16[1,512,1024]{2,1,0:T(8,128)(2,1)} %param.10) | copy-start | bytes 3145732
  40.5 4.3 copy-start.5
  45.7 26.8 %collective-permute-start = (bf16[256,1024]{1,0:T(8,128)(2,1)S(1)}, bf16[256,1024]{1,0:T(8,128)(2,1)S(1)}, u32[]{:S(2)}, u32[]{:S(2)}) collective-permute-start(bf16[256,1024]{1,0:T(8,128)(2,1)S(1)} %get-tuple-element.113), channel_id=1, source_target_pairs={{0,8},{8,16},{16,24},{24,32},{32,40},{40,48},{48,56},{56,64},{64,7... | collective-permute-start | bytes 1572872 | tf_op jit(solution)/shard_map/ppermute | solution.py:29
  47.8 24.8 %collective-permute-start.1 = (bf16[256,1024]{1,0:T(8,128)(2,1)S(1)}, bf16[256,1024]{1,0:T(8,128)(2,1)}, u32[]{:S(2)}, u32[]{:S(2)}) collective-permute-start(bf16[256,1024]{1,0:T(8,128)(2,1)S(1)} %get-tuple-element.113), channel_id=1, source_target_pairs={{0,120},{8,0},{16,8},{24,16},{32,24},{40,32},{48,40},{56,48},{64,5... | collective-permute-start | bytes 1572872 | tf_op jit(solution)/shard_map/ppermute | solution.py:34
  72.5 0.8 copy-start.8
  72.5 19.4 %collective-permute-start.2 = (bf16[256,1024]{1,0:T(8,128)(2,1)S(1)}, bf16[256,1024]{1,0:T(8,128)(2,1)}, u32[]{:S(2)}, u32[]{:S(2)}) collective-permute-start(bf16[256,1024]{1,0:T(8,128)(2,1)S(1)} %collective-permute-done), channel_id=1, source_target_pairs={{0,8},{8,16},{16,24},{24,32},{32,40},{40,48},{48,56},{56,64},{64,7... | collective-permute-start | bytes 1572872 | tf_op jit(solution)/shard_map/ppermute | solution.py:29
  73.3 22.9 %collective-permute-start.3 = (bf16[256,1024]{1,0:T(8,128)(2,1)}, bf16[256,1024]{1,0:T(8,128)(2,1)}, u32[]{:S(2)}, u32[]{:S(2)}) collective-permute-start(bf16[256,1024]{1,0:T(8,128)(2,1)} %collective-permute-done.1), channel_id=1, source_target_pairs={{0,120},{8,0},{16,8},{24,16},{32,24},{40,32},{48,40},{56,48},{64,5... | collective-permute-start | bytes 1572872 | tf_op jit(solution)/shard_map/ppermute | solution.py:34
  92.0 27.3 %collective-permute-start.4 = (bf16[256,1024]{1,0:T(8,128)(2,1)}, bf16[256,1024]{1,0:T(8,128)(2,1)}, u32[]{:S(2)}, u32[]{:S(2)}) collective-permute-start(bf16[256,1024]{1,0:T(8,128)(2,1)} %collective-permute-done.2), channel_id=1, source_target_pairs={{0,8},{8,16},{16,24},{24,32},{32,40},{40,48},{48,56},{56,64},{64,7... | collective-permute-start | bytes 1572872 | tf_op jit(solution)/shard_map/ppermute | solution.py:29
  96.2 27.0 %collective-permute-start.5 = (bf16[256,1024]{1,0:T(8,128)(2,1)}, bf16[256,1024]{1,0:T(8,128)(2,1)}, u32[]{:S(2)}, u32[]{:S(2)}) collective-permute-start(bf16[256,1024]{1,0:T(8,128)(2,1)} %collective-permute-done.3), channel_id=1, source_target_pairs={{0,120},{8,0},{16,8},{24,16},{32,24},{40,32},{48,40},{56,48},{64,5... | collective-permute-start | bytes 1572872 | tf_op jit(solution)/shard_map/ppermute | solution.py:34
  119.3 25.0 %collective-permute-start.6 = (bf16[256,1024]{1,0:T(8,128)(2,1)}, bf16[256,1024]{1,0:T(8,128)(2,1)}, u32[]{:S(2)}, u32[]{:S(2)}) collective-permute-start(bf16[256,1024]{1,0:T(8,128)(2,1)} %collective-permute-done.4), channel_id=1, source_target_pairs={{0,8},{8,16},{16,24},{24,32},{32,40},{40,48},{48,56},{56,64},{64,7... | collective-permute-start | bytes 1572872 | tf_op jit(solution)/shard_map/ppermute | solution.py:29
  123.2 23.1 %collective-permute-start.7 = (bf16[256,1024]{1,0:T(8,128)(2,1)}, bf16[256,1024]{1,0:T(8,128)(2,1)}, u32[]{:S(2)}, u32[]{:S(2)}) collective-permute-start(bf16[256,1024]{1,0:T(8,128)(2,1)} %collective-permute-done.5), channel_id=1, source_target_pairs={{0,120},{8,0},{16,8},{24,16},{32,24},{40,32},{48,40},{56,48},{64,5... | collective-permute-start | bytes 1572872 | tf_op jit(solution)/shard_map/ppermute | solution.py:34
  144.3 14.9 %collective-permute-start.8 = (bf16[256,1024]{1,0:T(8,128)(2,1)}, bf16[256,1024]{1,0:T(8,128)(2,1)}, u32[]{:S(2)}, u32[]{:S(2)}) collective-permute-start(bf16[256,1024]{1,0:T(8,128)(2,1)} %collective-permute-done.6), channel_id=1, source_target_pairs={{0,8},{8,16},{16,24},{24,32},{32,40},{40,48},{48,56},{56,64},{64,7... | collective-permute-start | bytes 1572872 | tf_op jit(solution)/shard_map/ppermute | solution.py:29
  146.3 27.8 %collective-permute-start.9 = (bf16[256,1024]{1,0:T(8,128)(2,1)}, bf16[256,1024]{1,0:T(8,128)(2,1)}, u32[]{:S(2)}, u32[]{:S(2)}) collective-permute-start(bf16[256,1024]{1,0:T(8,128)(2,1)} %collective-permute-done.7), channel_id=1, source_target_pairs={{0,120},{8,0},{16,8},{24,16},{32,24},{40,32},{48,40},{56,48},{64,5... | collective-permute-start | bytes 1572872 | tf_op jit(solution)/shard_map/ppermute | solution.py:34
  159.2 21.8 %collective-permute-start.10 = (bf16[256,1024]{1,0:T(8,128)(2,1)}, bf16[256,1024]{1,0:T(8,128)(2,1)}, u32[]{:S(2)}, u32[]{:S(2)}) collective-permute-start(bf16[256,1024]{1,0:T(8,128)(2,1)} %collective-permute-done.8), channel_id=1, source_target_pairs={{0,8},{8,16},{16,24},{24,32},{32,40},{40,48},{48,56},{56,64},{64,7... | collective-permute-start | bytes 1572872 | tf_op jit(solution)/shard_map/ppermute | solution.py:29
  159.9 405.7 %all-to-all-start = ((bf16[8,2,128]{2,1,0:T(2,128)(2,1)}), bf16[8,2,128]{2,1,0:T(2,128)(2,1)S(1)}, u32[]{:S(2)}, u32[]{:S(2)}) async-start(bf16[8,2,128]{2,1,0:T(2,128)(2,1)} %select_convert_fusion), calls=%async_computation | async-start | bytes 8192 | tf_op jit(solution)/shard_map/all_to_all | solution.py:151
  174.1 16.7 %collective-permute-start.11 = (bf16[256,1024]{1,0:T(8,128)(2,1)}, bf16[256,1024]{1,0:T(8,128)(2,1)S(1)}, u32[]{:S(2)}, u32[]{:S(2)}) collective-permute-start(bf16[256,1024]{1,0:T(8,128)(2,1)} %collective-permute-done.9), channel_id=1, source_target_pairs={{0,120},{8,0},{16,8},{24,16},{32,24},{40,32},{48,40},{56,48},{64,5... | collective-permute-start | bytes 1572872 | tf_op jit(solution)/shard_map/ppermute | solution.py:34
  181.1 17.1 %collective-permute-start.12 = (bf16[256,1024]{1,0:T(8,128)(2,1)}, bf16[256,1024]{1,0:T(8,128)(2,1)S(1)}, u32[]{:S(2)}, u32[]{:S(2)}) collective-permute-start(bf16[256,1024]{1,0:T(8,128)(2,1)} %collective-permute-done.10), channel_id=1, source_target_pairs={{0,8},{8,16},{16,24},{24,32},{32,40},{40,48},{48,56},{56,64},{64,7... | collective-permute-start | bytes 1572872 | tf_op jit(solution)/shard_map/ppermute | solution.py:29
  190.8 15.9 %collective-permute-start.13 = (bf16[256,1024]{1,0:T(8,128)(2,1)S(1)}, bf16[256,1024]{1,0:T(8,128)(2,1)S(1)}, u32[]{:S(2)}, u32[]{:S(2)}) collective-permute-start(bf16[256,1024]{1,0:T(8,128)(2,1)S(1)} %collective-permute-done.11), channel_id=1, source_target_pairs={{0,120},{8,0},{16,8},{24,16},{32,24},{40,32},{48,40},{56,48},{64,5... | collective-permute-start | bytes 1572872 | tf_op jit(solution)/shard_map/ppermute | solution.py:34
  198.1 15.7 %collective-permute-start.14 = (bf16[256,1024]{1,0:T(8,128)(2,1)S(1)}, bf16[256,1024]{1,0:T(8,128)(2,1)S(1)}, u32[]{:S(2)}, u32[]{:S(2)}) collective-permute-start(bf16[256,1024]{1,0:T(8,128)(2,1)S(1)} %collective-permute-done.12), channel_id=1, source_target_pairs={{0,8},{8,16},{16,24},{24,32},{32,40},{40,48},{48,56},{56,64},{64,7... | collective-permute-start | bytes 1572872 | tf_op jit(solution)/shard_map/ppermute | solution.py:29
  553.3 4.7 copy-start.9
  556.6 1.4 copy-start.2
  565.6 55.4 %all-to-all-start.1 = ((bf16[8,2,128,1024]{3,2,1,0:T(8,128)(2,1)}), bf16[8,2,128,1024]{3,2,1,0:T(8,128)(2,1)}, u32[]{:S(2)}, u32[]{:S(2)}) async-start(bf16[8,2,128,1024]{3,2,1,0:T(8,128)(2,1)} %select_select_fusion), calls=%async_computation.1 | async-start | bytes 8388608 | tf_op jit(solution)/shard_map/all_to_all | solution.py:150
Sparse Core Ops, SparseCore 0:
  33.3 109.3 all-gather.1
